TPU v7x, 32 devices: a whole 2x2x4 slice. The times are simulated.
32 devices in a mesh: img: 4 (over y, x), rows: 8 (over z, core).
Axes of the slice: x: 2, y: 2, z: 4, core: 2. Of those that a mesh axis runs over, the one named last changes fastest.
Arguments:
- features: bfloat16 [8, 16, 256, 512], P('img', 'rows'), parts along dimension 0, may hold values from -100 to 100
- conv_first: bfloat16 [3, 3, 512, 512], replicated, may hold values from -0.09375 to 0.09375
- conv_second: bfloat16 [3, 3, 512, 512], replicated, may hold values from -0.09375 to 0.09375
- query_weight: bfloat16 [512, 512], replicated, may hold values from -0.25 to 0.25
- key_weight: bfloat16 [512, 512], replicated, may hold values from -0.25 to 0.25
- value_weight: bfloat16 [512, 512], replicated, may hold values from -0.25 to 0.25
- output_weight: bfloat16 [512, 512], replicated, may hold values from -0.25 to 0.25
- time_weight: bfloat16 [256, 1024], replicated, may hold values from -0.375 to 0.375
- norm_gains: float32 [3, 512], replicated, may hold values from 0.1 to 1.9
- norm_shifts: float32 [3, 512], replicated, may hold values from -3 to 3
- text_states: bfloat16 [8, 128, 512], P('img'), parts along dimension 0, may hold values from -500 to 500
- timestep: int32 [8], P('img'), parts along dimension 0, may hold values from 0 to 999
- aug_level: int32 [8], P('img'), parts along dimension 0, may hold values from 0 to 999
- text_length: int32 [8], P('img'), parts along dimension 0, may hold values from 2 to 128
Outputs:
- block_output: bfloat16 [8, 16, 256, 512], P('img', 'rows'), parts along dimension 0
There are 4 independent parts, one for each index of `img`. A program takes and returns all parts, laid end to end along the dimension named above; an argument that names none is the same for every part. Nothing has to cross between parts.
All inputs are finite; a program needn't handle non-finite values.
Results may differ from a plain program's by a relative error of at most 0.035.
Values may be sent and summed in bfloat16 or wider, within the bound.
A program may use at most 128 MiB of HBM per device.

v0:
```python
import math

import jax
import jax.numpy as jnp
from jax import lax
from jax.sharding import PartitionSpec as P

GROUPS = 32
HEADS = 8
HEAD_DIM = 64
TFREQ = 64
TXT = 128


EPSILON = 1e-05


def padded_2(block, sides, width):
    for axis, dim in sides:
        count = lax.axis_size(axis)
        forward = [(i, i + 1) for i in range(count - 1)]
        backward = [(target, source) for source, target in forward]
        low = lax.ppermute(
            lax.slice_in_dim(block, block.shape[dim] - width, None, axis=dim), axis, forward
        )
        high = lax.ppermute(lax.slice_in_dim(block, 0, width, axis=dim), axis, backward)
        block = jnp.concatenate([low, block, high], axis=dim)
    return block


def to_groups(per_channel):
    return per_channel.reshape(per_channel.shape[0], GROUPS, -1).sum(axis=2)


def to_channels(per_group, channels):
    return jnp.repeat(per_group, channels // GROUPS, axis=1)[:, None, None, :]


def normalize(values, cells_count):
    channels = values.shape[3]
    totals, squares = lax.psum(
        (to_groups(values.sum(axis=(1, 2))), to_groups(jnp.square(values).sum(axis=(1, 2)))), "rows"
    )
    group_mean = totals / cells_count
    spread = squares / cells_count - group_mean * group_mean
    return (values - to_channels(group_mean, channels)) * to_channels(
        lax.rsqrt(spread + EPSILON), channels
    )


def sinusoid(steps):
    freqs = jnp.exp(jnp.arange(TFREQ, dtype=jnp.float32) * (-math.log(10000.0) / TFREQ))
    angles = steps.astype(jnp.float32)[:, None] * freqs[None, :]
    return jnp.concatenate([jnp.sin(angles), jnp.cos(angles)], axis=1)


def conditioning(timestep, aug_level, time_weight, channels):
    embedded = jnp.concatenate([sinusoid(timestep), sinusoid(aug_level)], axis=1).astype(
        jnp.bfloat16
    )
    film_terms = jnp.dot(embedded, time_weight, preferred_element_type=jnp.float32)
    return (film_terms[:, None, None, :channels], film_terms[:, None, None, channels:])


def convolve(padded_rows, weight):
    images, rows_in, col_count, channels = padded_rows.shape
    out_rows = rows_in - 2
    padded = jnp.pad(padded_rows, ((0, 0), (0, 0), (1, 1), (0, 0)))
    widened = jnp.concatenate(
        [
            padded[:, :, 0:col_count],
            padded[:, :, 1 : col_count + 1],
            padded[:, :, 2 : col_count + 2],
        ],
        axis=3,
    )
    stacked = weight.reshape(3, 3 * channels, channels)
    total = jnp.zeros((images * out_rows * col_count, channels), jnp.float32)
    for offset in range(3):
        window = widened[:, offset : offset + out_rows].reshape(-1, 3 * channels)
        total = total + jnp.dot(window, stacked[offset], preferred_element_type=jnp.float32)
    return total.reshape(images, out_rows, col_count, channels)


def with_rims(block):
    return padded_2(block, (("rows", 1),), 1)


def cross_attend(
    normed, text_states, text_length, query_weight, key_weight, value_weight, output_weight
):
    images, rows_here, col_count, channels = normed.shape
    queries = jnp.dot(
        normed.reshape(-1, channels), query_weight, preferred_element_type=jnp.float32
    ).astype(jnp.bfloat16)
    queries = queries.reshape(images, rows_here * col_count, HEADS, HEAD_DIM)
    flat_text = text_states.reshape(-1, channels)
    key_rows = jnp.dot(flat_text, key_weight, preferred_element_type=jnp.float32).astype(
        jnp.bfloat16
    )
    key_rows = key_rows.reshape(images, TXT, HEADS, HEAD_DIM)
    value_rows = jnp.dot(flat_text, value_weight, preferred_element_type=jnp.float32).astype(
        jnp.bfloat16
    )
    value_rows = value_rows.reshape(images, TXT, HEADS, HEAD_DIM)
    scores = jnp.einsum(
        "iqhd,ikhd->ihqk", queries, key_rows, preferred_element_type=jnp.float32
    ) * HEAD_DIM ** (-0.5)
    inside = (jnp.arange(TXT, dtype=jnp.int32)[None, :] < text_length[:, None])[:, None, None, :]
    scores = jnp.where(inside, scores, -jnp.inf)
    highest = jnp.max(scores, axis=3, keepdims=True)
    raised = jnp.exp(scores - highest)
    attention = (raised / jnp.sum(raised, axis=3, keepdims=True)).astype(jnp.bfloat16)
    mixed_heads = jnp.einsum(
        "ihqk,ikhd->iqhd", attention, value_rows, preferred_element_type=jnp.float32
    ).astype(jnp.bfloat16)
    projected = jnp.dot(
        mixed_heads.reshape(-1, channels), output_weight, preferred_element_type=jnp.float32
    )
    return projected.reshape(images, rows_here, col_count, channels)


def shards(
    features,
    conv_first,
    conv_second,
    query_weight,
    key_weight,
    value_weight,
    output_weight,
    time_weight,
    norm_gains,
    norm_shifts,
    text_states,
    timestep,
    aug_level,
    text_length,
):
    band_rows = features.shape[1]
    band_count = lax.axis_size("rows")
    channels = features.shape[3]
    cells_count = band_rows * band_count * features.shape[2] * (channels // GROUPS)
    film_scale, film_shift = conditioning(timestep, aug_level, time_weight, channels)
    residual = features.astype(jnp.float32)
    first_act = jax.nn.silu(
        normalize(residual, cells_count) * norm_gains[0] + norm_shifts[0]
    ).astype(jnp.bfloat16)
    hidden_one = convolve(with_rims(first_act), conv_first)
    second_core = jax.nn.silu(
        (normalize(hidden_one, cells_count) * norm_gains[1] + norm_shifts[1]) * (1.0 + film_scale)
        + film_shift
    ).astype(jnp.bfloat16)
    second_act = with_rims(second_core)
    block_out = (residual + convolve(second_act, conv_second)).astype(jnp.bfloat16)
    normed = (
        normalize(block_out.astype(jnp.float32), cells_count) * norm_gains[2] + norm_shifts[2]
    ).astype(jnp.bfloat16)
    attended = cross_attend(
        normed, text_states, text_length, query_weight, key_weight, value_weight, output_weight
    )
    return (block_out.astype(jnp.float32) + attended).astype(jnp.bfloat16)


def solution(mesh):
    placed = (
        P("img", "rows", None, None),
        P(),
        P(),
        P(),
        P(),
        P(),
        P(),
        P(),
        P(),
        P(),
        P("img", None, None),
        P("img"),
        P("img"),
        P("img"),
    )
    return jax.shard_map(
        shards, mesh=mesh, in_specs=placed, out_specs=P("img", "rows", None, None), check_vma=False
    )
```

profile of v0, /device:TPU:0, one launch (start us, length us, event | category | flops | bytes accessed | tf_op | source)
XLA Modules:
  0.0 112.2 jit_solution(12030422332259151185)
XLA Ops:
  0.0 1.6 %convert_reduce_fusion.1 = (f32[2,512]{1,0:T(2,128)S(1)}, f32[2,512]{1,0:T(2,128)S(1)}) fusion(bf16[2,2,256,512]{3,2,1,0:T(8,128)(2,1)} %param.14), kind=kLoop, calls=%fused_computation.16 | loop fusion | flops 2095104 | bytes 1056768 | tf_op jit(solution)/shard_map/reduce_sum | solution.py:42
  2.0 18.1 %all-reduce.4 = (f32[2,32]{1,0:T(2,128)S(1)}, f32[2,32]{1,0:T(2,128)S(1)}) all-reduce(f32[2,32]{1,0:T(2,128)S(1)} %reduce_sum.120, f32[2,32]{1,0:T(2,128)S(1)} %reduce_sum.118), channel_id=1, replica_groups=mesh['img'=4,'rows'=8] {'rows'}, use_global_device_ids=true, to_apply=%region_5.0 | all-reduce | flops 128 | bytes 1024 | tf_op jit(solution)/shard_map/psum | solution.py:41
  20.2 0.1 mul.127
  20.4 0.8 fusion.67
  21.2 0.8 fusion.68
  22.1 0.7 fusion.16
  22.8 1.0 fusion.66
  23.9 1.3 %collective-permute-start = (bf16[2,1,256,512]{3,2,1,0:T(8,128)(2,1)}, bf16[2,1,256,512]{3,2,1,0:T(8,128)(2,1)S(1)}, u32[]{:S(2)}, u32[]{:S(2)}) collective-permute-start(bf16[2,1,256,512]{3,2,1,0:T(8,128)(2,1)} %get-tuple-element.36), channel_id=1, source_target_pairs={{0,1},{1,2},{2,3},{3,4},{4,5},{5,6},{6,7},{8,9},{9,10},{10,11},{11... | collective-permute-start | bytes 1572872 | tf_op jit(solution)/shard_map/ppermute | solution.py:23
  25.2 1.3 %collective-permute-start.1 = (bf16[2,1,256,512]{3,2,1,0:T(8,128)(2,1)}, bf16[2,1,256,512]{3,2,1,0:T(8,128)(2,1)}, u32[]{:S(2)}, u32[]{:S(2)}) collective-permute-start(bf16[2,1,256,512]{3,2,1,0:T(8,128)(2,1)} %get-tuple-element.37), channel_id=1, source_target_pairs={{1,0},{2,1},{3,2},{4,3},{5,4},{6,5},{7,6},{9,8},{10,9},{11,10},{12... | collective-permute-start | bytes 1572872 | tf_op jit(solution)/shard_map/ppermute | solution.py:26
  26.6 0.3 convolution_convert_fusion.1
  26.9 1.1 reshape.138
  27.9 1.4 %convolution_convert_fusion.2 = bf16[256,512]{1,0:T(8,128)(2,1)S(1)} fusion(bf16[256,512]{1,0:T(8,128)(2,1)} %bitcast.87, bf16[512,512]{1,0:T(8,128)(2,1)} %param.19), kind=kOutput, calls=%fused_computation.64 | convolution fusion | flops 134348800 | bytes 1048576 | tf_op jit(solution)/shard_map/dot_general | solution.py:102
  29.4 1.1 reshape.136
  30.5 0.1 fusion.43
  30.6 1.3 %fusion.47 = f32[2,1024]{1,0:T(2,128)S(1)} fusion(bf16[256,1024]{1,0:T(8,128)(2,1)} %param.21, bf16[2,64]{1,0:T(2,128)(2,1)S(1)} %get-tuple-element.56, bf16[2,64]{1,0:T(2,128)(2,1)S(1)} %get-tuple-element.57, bf16[2,64]{1,0:T(2,128)(2,1)S(1)} %get-tuple-element.51, bf16[2,64]{1,0:T(2,128)(2,1)S(1)} %get-tuple-element.50), kind=kOutput, calls=%fused_computation.78 | convolution fusion | flops 1052672 | bytes 533504 | tf_op jit(solution)/shard_map/dot_general | solution.py:61
  31.9 2.7 %fusion.62 = (bf16[1,3,512,512]{3,2,1,0:T(8,128)(2,1)S(1)}, bf16[1,3,512,512]{3,2,1,0:T(8,128)(2,1)S(1)}, bf16[1,3,512,512]{3,2,1,0:T(8,128)(2,1)S(1)}) fusion(bf16[3,3,512,512]{3,2,1,0:T(8,128)(2,1)} %param.15), kind=kLoop, calls=%fused_computation.100 | loop fusion | bytes 9437184 | tf_op jit(solution)/shard_map/slice | solution.py:81
  34.5 1.6 %fusion.7 = bf16[2,4,258,512]{3,2,1,0:T(8,128)(2,1)S(1)} fusion(bf16[2,1,256,512]{3,2,1,0:T(8,128)(2,1)} %collective-permute-done.1, bf16[2,2,256,512]{3,2,1,0:T(8,128)(2,1)S(1)} %fusion.16, bf16[2,1,256,512]{3,2,1,0:T(8,128)(2,1)S(1)} %collective-permute-done), kind=kLoop, calls=%fused_computation.24 | loop fusion | flops 12681216 | bytes 4210688 | tf_op jit(solution)/shard_map/concatenate | solution.py:27
  36.1 0.7 fusion.64
  36.8 2.4 %pad_maximum_fusion = bf16[2,4,256,1536]{3,2,1,0:T(8,128)(2,1)S(1)} fusion(bf16[2,4,256,512]{3,2,1,0:T(8,128)(2,1)S(1)} %get-tuple-element.33, bf16[2,1,256,512]{3,2,1,0:T(8,128)(2,1)} %collective-permute-done.1, bf16[2,2,256,512]{3,2,1,0:T(8,128)(2,1)S(1)} %fusion.16, bf16[2,1,256,512]{3,2,1,0:T(8,128)(2,1)S(1)} %collective-permute-done, ...), kind=kLoop, calls=%fused_computation.3 | loop fusion | flops 31457280 | bytes 12582912 | tf_op jit(solution)/shard_map/concatenate | solution.py:69
  39.2 1.1 %fusion.60 = (bf16[2,2,256,1536]{3,2,1,0:T(8,128)(2,1)S(1)}, bf16[2,2,256,1536]{3,2,1,0:T(8,128)(2,1)S(1)}, bf16[2,2,256,1536]{3,2,1,0:T(8,128)(2,1)S(1)}) fusion(bf16[2,4,256,1536]{3,2,1,0:T(8,128)(2,1)S(1)} %pad_maximum_fusion), kind=kLoop, calls=%fused_computation.98 | loop fusion | bytes 18874368 | tf_op jit(solution)/shard_map/slice | solution.py:80
  40.4 1.8 %fusion.70 = f32[1024,512]{1,0:T(8,128)S(1)} fusion(bf16[1024,1536]{1,0:T(8,128)(2,1)S(1)} %bitcast.78, bf16[1536,512]{1,0:T(8,128)(2,1)S(1)} %bitcast.84), kind=kOutput, calls=%fused_computation.108 | convolution fusion | flops 1610612736 | bytes 6815744 | tf_op jit(solution)/shard_map/dot_general | solution.py:81
  42.1 1.8 %fusion.71 = f32[1024,512]{1,0:T(8,128)S(1)} fusion(bf16[1024,1536]{1,0:T(8,128)(2,1)S(1)} %bitcast.76, bf16[1536,512]{1,0:T(8,128)(2,1)S(1)} %bitcast.82), kind=kOutput, calls=%fused_computation.109 | convolution fusion | flops 1610612736 | bytes 6815744 | tf_op jit(solution)/shard_map/dot_general | solution.py:81
  43.9 3.3 %bitcast_reduce_fusion = (f32[2,512]{1,0:T(2,128)S(1)}, f32[2,512]{1,0:T(2,128)S(1)}, f32[1024,512]{1,0:T(8,128)}) fusion(bf16[1024,1536]{1,0:T(8,128)(2,1)S(1)} %bitcast.74, bf16[1536,512]{1,0:T(8,128)(2,1)S(1)} %bitcast.80, f32[1024,512]{1,0:T(8,128)S(1)} %fusion.70, f32[1024,512]{1,0:T(8,128)S(1)} %fusion.71), kind=kOutput, calls=%fused_computation.46 | convolution fusion | flops 1613232128 | bytes 11018240 | tf_op jit(solution)/shard_map/dot_general | solution.py:81
  47.5 15.6 %all-reduce.3 = (f32[2,32]{1,0:T(2,128)S(1)}, f32[2,32]{1,0:T(2,128)S(1)}) all-reduce(f32[2,32]{1,0:T(2,128)S(1)} %reduce_sum.124, f32[2,32]{1,0:T(2,128)S(1)} %reduce_sum.122), channel_id=1, replica_groups=mesh['img'=4,'rows'=8] {'rows'}, use_global_device_ids=true, to_apply=%region_11.12 | all-reduce | flops 128 | bytes 1024 | tf_op jit(solution)/shard_map/psum | solution.py:41
  63.2 0.1 mul.135
  63.5 2.4 %multiply_convert_fusion = bf16[2,2,256,512]{3,2,1,0:T(8,128)(2,1)S(1)} fusion(f32[1024,512]{1,0:T(8,128)} %get-tuple-element.58, f32[2,512]{1,0:T(2,128)S(1)} %get-tuple-element.45, f32[2,512]{1,0:T(2,128)S(1)} %get-tuple-element.44, f32[512]{0:T(512)S(1)} %bitcast.90, f32[512]{0:T(512)S(1)} %bitcast.89, f32[2,512]{1,0:T(2,128)S(1)} %mul.135, ...), kind=kLoop, calls=%fused_computation.56 | loop fusion | flops 5767168 | bytes 3166208 | tf_op jit(solution)/shard_map/convert_element_type | solution.py:152
  65.9 1.3 %collective-permute-start.2 = (bf16[2,1,256,512]{3,2,1,0:T(8,128)(2,1)S(1)}, bf16[2,1,256,512]{3,2,1,0:T(8,128)(2,1)S(1)}, u32[]{:S(2)}, u32[]{:S(2)}) collective-permute-start(bf16[2,1,256,512]{3,2,1,0:T(8,128)(2,1)S(1)} %get-tuple-element.34), channel_id=1, source_target_pairs={{0,1},{1,2},{2,3},{3,4},{4,5},{5,6},{6,7},{8,9},{9,10},{10,11},{11... | collective-permute-start | bytes 1572872 | tf_op jit(solution)/shard_map/ppermute | solution.py:23
  67.3 1.5 %collective-permute-start.3 = (bf16[2,1,256,512]{3,2,1,0:T(8,128)(2,1)S(1)}, bf16[2,1,256,512]{3,2,1,0:T(8,128)(2,1)S(1)}, u32[]{:S(2)}, u32[]{:S(2)}) collective-permute-start(bf16[2,1,256,512]{3,2,1,0:T(8,128)(2,1)S(1)} %get-tuple-element.35), channel_id=1, source_target_pairs={{1,0},{2,1},{3,2},{4,3},{5,4},{6,5},{7,6},{9,8},{10,9},{11,10},{12... | collective-permute-start | bytes 1572872 | tf_op jit(solution)/shard_map/ppermute | solution.py:26
  68.8 2.7 %fusion.61 = (bf16[1,3,512,512]{3,2,1,0:T(8,128)(2,1)S(1)}, bf16[1,3,512,512]{3,2,1,0:T(8,128)(2,1)S(1)}, bf16[1,3,512,512]{3,2,1,0:T(8,128)(2,1)S(1)}) fusion(bf16[3,3,512,512]{3,2,1,0:T(8,128)(2,1)} %param.16), kind=kLoop, calls=%fused_computation.99 | loop fusion | bytes 9437184 | tf_op jit(solution)/shard_map/slice | solution.py:81
  71.5 0.6 select_maximum_fusion
  72.1 0.7 fusion.63
  72.8 0.8 pad_maximum_fusion.1
  73.6 1.1 %fusion.59 = (bf16[2,2,256,1536]{3,2,1,0:T(8,128)(2,1)S(1)}, bf16[2,2,256,1536]{3,2,1,0:T(8,128)(2,1)S(1)}, bf16[2,2,256,1536]{3,2,1,0:T(8,128)(2,1)S(1)}) fusion(bf16[2,4,256,1536]{3,2,1,0:T(8,128)(2,1)S(1)} %pad_maximum_fusion.1), kind=kLoop, calls=%fused_computation.97 | loop fusion | bytes 18874368 | tf_op jit(solution)/shard_map/slice | solution.py:80
  74.7 1.8 %fusion.73 = f32[1024,512]{1,0:T(8,128)S(1)} fusion(bf16[1024,1536]{1,0:T(8,128)(2,1)S(1)} %bitcast.79, bf16[1536,512]{1,0:T(8,128)(2,1)S(1)} %bitcast.85), kind=kOutput, calls=%fused_computation.111 | convolution fusion | flops 1610612736 | bytes 6815744 | tf_op jit(solution)/shard_map/dot_general | solution.py:81
  76.5 1.8 %fusion.72 = f32[1024,512]{1,0:T(8,128)S(1)} fusion(bf16[1024,1536]{1,0:T(8,128)(2,1)S(1)} %bitcast.77, bf16[1536,512]{1,0:T(8,128)(2,1)S(1)} %bitcast.83), kind=kOutput, calls=%fused_computation.110 | convolution fusion | flops 1610612736 | bytes 6815744 | tf_op jit(solution)/shard_map/dot_general | solution.py:81
  78.3 2.2 %convert_reduce_fusion = (f32[2,512]{1,0:T(2,128)S(1)}, f32[2,512]{1,0:T(2,128)S(1)}, bf16[2,2,256,512]{3,2,1,0:T(8,128)(2,1)S(1)}) fusion(bf16[2,2,256,512]{3,2,1,0:T(8,128)(2,1)S(1)} %copy-done.1, bf16[1536,512]{1,0:T(8,128)(2,1)S(1)} %bitcast.81, bf16[1024,1536]{1,0:T(8,128)(2,1)S(1)} %bitcast.75, f32[1024,512]{1,0:T(8,128)S(1)} %fusion.72, ...), kind=kOutput, calls=%fused_computation.12 | convolution fusion | flops 1615329280 | bytes 11018240 | tf_op jit(solution)/shard_map/dot_general | solution.py:81
  80.8 18.5 %all-reduce.2 = (f32[2,32]{1,0:T(2,128)S(1)}, f32[2,32]{1,0:T(2,128)S(1)}) all-reduce(f32[2,32]{1,0:T(2,128)S(1)} %reduce_sum.128, f32[2,32]{1,0:T(2,128)S(1)} %reduce_sum.126), channel_id=1, replica_groups=mesh['img'=4,'rows'=8] {'rows'}, use_global_device_ids=true, to_apply=%region_17.18 | all-reduce | flops 128 | bytes 1024 | tf_op jit(solution)/shard_map/psum | solution.py:41
  99.4 0.1 mul.151
  99.7 0.4 fusion.22
  100.1 1.7 %convolution_convert_fusion = bf16[1024,512]{1,0:T(8,128)(2,1)} fusion(bf16[1024,512]{1,0:T(8,128)(2,1)S(1)} %bitcast.86, bf16[512,512]{1,0:T(8,128)(2,1)S(1)} %copy-done), kind=kOutput, calls=%fused_computation.61 | convolution fusion | flops 537395200 | bytes 2621440 | tf_op jit(solution)/shard_map/dot_general | solution.py:93
  101.8 2.8 %reshape.137 = bf16[2,512,8,64]{3,2,1,0:T(8,128)(2,1)S(1)} reshape(bf16[1024,512]{1,0:T(8,128)(2,1)} %convolution_convert_fusion) | data formatting | bytes 2097152 | tf_op jit(solution)/shard_map/reshape | solution.py:96
  104.7 0.7 fusion.25
  105.4 1.6 %fusion.69 = (f32[2,8,512]{2,1,0:T(8,128)S(1)}, f32[2,8,512,128]{2,3,1,0:T(8,128)S(1)}) fusion(f32[2,8,512,128]{2,3,1,0:T(8,128)S(1)} %fusion.25, pred[2,128]{1,0:T(4,128)(4,1)S(1)} %iota_compare_fusion.2), kind=kOutput, calls=%fused_computation.107 | output fusion | flops 6291583 | bytes 8421632 | tf_op jit(solution)/shard_map/sub | solution.py:112
  107.0 0.5 fusion.38
  107.6 1.1 %dot_general.53 = bf16[2,2,256,512]{2,1,3,0:T(2,128)(2,1)} reshape(bf16[2,512,8,64]{1,3,2,0:T(8,128)(2,1)S(1)} %fusion.38) | data formatting | bytes 2097152 | tf_op jit(solution)/shard_map/dot_general | solution.py:117
  108.7 0.4 copy-done.4
  109.1 0.2 copy-done.8
  109.3 2.9 %fusion.24 = bf16[2,2,256,512]{3,2,1,0:T(8,128)(2,1)} fusion(bf16[2,2,256,512]{3,2,1,0:T(8,128)(2,1)S(1)} %copy-done.4, bf16[2,2,256,512]{2,1,3,0:T(2,128)(2,1)} %dot_general.53, bf16[512,512]{1,0:T(8,128)(2,1)S(1)} %copy-done.8), kind=kOutput, calls=%fused_computation.41 | convolution fusion | flops 538443776 | bytes 3670016 | tf_op jit(solution)/shard_map/dot_general | solution.py:117
  (56 shorter events, 2.0 us)
Async XLA Ops:
  0.0 100.1 %copy-start = (bf16[512,512]{1,0:T(8,128)(2,1)S(1)}, bf16[512,512]{1,0:T(8,128)(2,1)}, u32[]{:S(2)}) copy-start(bf16[512,512]{1,0:T(8,128)(2,1)} %param.17) | copy-start | bytes 1572868
  0.0 22.1 %copy-start.1 = (bf16[2,2,256,512]{3,2,1,0:T(8,128)(2,1)S(1)}, bf16[2,2,256,512]{3,2,1,0:T(8,128)(2,1)}, u32[]{:S(2)}) copy-start(bf16[2,2,256,512]{3,2,1,0:T(8,128)(2,1)} %param.14) | copy-start | bytes 3145732
  22.1 4.4 %copy-start.9 = (s32[2]{0:T(128)S(1)}, s32[2]{0:T(128)}, u32[]{:S(2)}) copy-start(s32[2]{0:T(128)} %param.25) | copy-start | bytes 28
  22.1 4.5 %copy-start.10 = (s32[2]{0:T(128)S(1)}, s32[2]{0:T(128)}, u32[]{:S(2)}) copy-start(s32[2]{0:T(128)} %param.26) | copy-start | bytes 28
  22.1 4.5 %copy-start.5 = (bf16[2,128,512]{2,1,0:T(8,128)(2,1)S(1)}, bf16[2,128,512]{2,1,0:T(8,128)(2,1)}, u32[]{:S(2)}) copy-start(bf16[2,128,512]{2,1,0:T(8,128)(2,1)} %param.24) | copy-start | bytes 786436
  22.1 4.5 %copy-start.7 = (bf16[512,512]{1,0:T(8,128)(2,1)S(1)}, bf16[512,512]{1,0:T(8,128)(2,1)}, u32[]{:S(2)}) copy-start(bf16[512,512]{1,0:T(8,128)(2,1)} %param.18) | copy-start | bytes 1572868
  23.9 10.6 %collective-permute-start = (bf16[2,1,256,512]{3,2,1,0:T(8,128)(2,1)}, bf16[2,1,256,512]{3,2,1,0:T(8,128)(2,1)S(1)}, u32[]{:S(2)}, u32[]{:S(2)}) collective-permute-start(bf16[2,1,256,512]{3,2,1,0:T(8,128)(2,1)} %get-tuple-element.36), channel_id=1, source_target_pairs={{0,1},{1,2},{2,3},{3,4},{4,5},{5,6},{6,7},{8,9},{9,10},{10,11},{11... | collective-permute-start | bytes 1572872 | tf_op jit(solution)/shard_map/ppermute | solution.py:23
  25.2 9.3 %collective-permute-start.1 = (bf16[2,1,256,512]{3,2,1,0:T(8,128)(2,1)}, bf16[2,1,256,512]{3,2,1,0:T(8,128)(2,1)}, u32[]{:S(2)}, u32[]{:S(2)}) collective-permute-start(bf16[2,1,256,512]{3,2,1,0:T(8,128)(2,1)} %get-tuple-element.37), channel_id=1, source_target_pairs={{1,0},{2,1},{3,2},{4,3},{5,4},{6,5},{7,6},{9,8},{10,9},{11,10},{12... | collective-permute-start | bytes 1572872 | tf_op jit(solution)/shard_map/ppermute | solution.py:26
  63.4 5.3 %copy-start.11 = (s32[2]{0:T(128)S(1)}, s32[2]{0:T(128)}, u32[]{:S(2)}) copy-start(s32[2]{0:T(128)} %param.27) | copy-start | bytes 28
  65.9 5.6 %collective-permute-start.2 = (bf16[2,1,256,512]{3,2,1,0:T(8,128)(2,1)S(1)}, bf16[2,1,256,512]{3,2,1,0:T(8,128)(2,1)S(1)}, u32[]{:S(2)}, u32[]{:S(2)}) collective-permute-start(bf16[2,1,256,512]{3,2,1,0:T(8,128)(2,1)S(1)} %get-tuple-element.34), channel_id=1, source_target_pairs={{0,1},{1,2},{2,3},{3,4},{4,5},{5,6},{6,7},{8,9},{9,10},{10,11},{11... | collective-permute-start | bytes 1572872 | tf_op jit(solution)/shard_map/ppermute | solution.py:23
  67.3 4.2 %collective-permute-start.3 = (bf16[2,1,256,512]{3,2,1,0:T(8,128)(2,1)S(1)}, bf16[2,1,256,512]{3,2,1,0:T(8,128)(2,1)S(1)}, u32[]{:S(2)}, u32[]{:S(2)}) collective-permute-start(bf16[2,1,256,512]{3,2,1,0:T(8,128)(2,1)S(1)} %get-tuple-element.35), channel_id=1, source_target_pairs={{1,0},{2,1},{3,2},{4,3},{5,4},{6,5},{7,6},{9,8},{10,9},{11,10},{12... | collective-permute-start | bytes 1572872 | tf_op jit(solution)/shard_map/ppermute | solution.py:26
  80.5 19.6 %copy-start.3 = (bf16[2,2,256,512]{3,2,1,0:T(8,128)(2,1)}, bf16[2,2,256,512]{3,2,1,0:T(8,128)(2,1)S(1)}, u32[]{:S(2)}) copy-start(bf16[2,2,256,512]{3,2,1,0:T(8,128)(2,1)S(1)} %get-tuple-element.17) | copy-start | bytes 3145732
  101.8 2.9 %copy-start.2 = (bf16[2,128,8,64]{3,2,1,0:T(8,128)(2,1)S(1)}, bf16[2,128,8,64]{3,2,1,0:T(8,128)(2,1)}, u32[]{:S(2)}) copy-start(bf16[2,128,8,64]{3,2,1,0:T(8,128)(2,1)} %reshape.138) | copy-start | bytes 786436
  105.4 1.6 %copy-start.6 = (bf16[2,128,8,64]{3,2,1,0:T(8,128)(2,1)S(1)}, bf16[2,128,8,64]{3,2,1,0:T(8,128)(2,1)}, u32[]{:S(2)}) copy-start(bf16[2,128,8,64]{3,2,1,0:T(8,128)(2,1)} %reshape.136) | copy-start | bytes 786436
  107.5 1.6 %copy-start.4 = (bf16[2,2,256,512]{3,2,1,0:T(8,128)(2,1)S(1)}, bf16[2,2,256,512]{3,2,1,0:T(8,128)(2,1)}, u32[]{:S(2)}) copy-start(bf16[2,2,256,512]{3,2,1,0:T(8,128)(2,1)} %copy-done.3) | copy-start | bytes 3145732
  107.5 1.7 %copy-start.8 = (bf16[512,512]{1,0:T(8,128)(2,1)S(1)}, bf16[512,512]{1,0:T(8,128)(2,1)}, u32[]{:S(2)}) copy-start(bf16[512,512]{1,0:T(8,128)(2,1)} %param.20) | copy-start | bytes 1572868
where the time goes:
time: 113 us; the launch traced here: 112 us
  blocking collectives  52.2 us (46%)
  matrix products  21.4 us (19%)
  local copies, waits for them, and re-layouts  19.9 us (18%)
  other arithmetic  12.9 us (11%)
  starting transfers between devices  5.4 us (5%)
    psum x3, blocking collectives, normalize(): lax.psum((to_groups(values.sum(axis=(1, 2))), to_groups(jnp.square(values...  52.2 us
    dot_general x6, matrix products, convolve(): jnp.dot(window, stacked[offset], preferred_element_type=jnp.float32)  12.6 us
    slice x2, local copies, waits for them, and re-layouts, convolve(): stacked[offset]  5.32 us
    concatenate x2, other arithmetic, convolve(): jnp.concatenate([padded[:, :, 0:col_count], padded[:, :, 1:col_count + 1]...  3.2 us
    dot_general x1, matrix products, cross_attend(): jnp.dot(mixed_heads.reshape(-1, channels), output_weight, preferred_eleme...  2.94 us
    reshape x1, local copies, waits for them, and re-layouts, cross_attend(): queries = queries.reshape(images, rows_here * col_count, HEADS, HEAD_DIM)  2.84 us
    ppermute x2, starting transfers between devices, padded_2(): lax.ppermute(lax.slice_in_dim(block, 0, width, axis=dim), axis, backward)  2.76 us
    ppermute x2, starting transfers between devices, padded_2(): lax.ppermute(lax.slice_in_dim(block, block.shape[dim] - width, None, axis...  2.63 us
  transfers between devices with their start and end apart: 4, of which 0 were waited for; matrix products, arithmetic and copies ran while one was open for 10% of the time, Pallas kernels for 0%

commit v1 on v0

v1 whole, which is shorter than its diff:
```python
import functools
import math

import jax
import jax.numpy as jnp
from jax import lax
from jax.experimental import pallas as pl
from jax.experimental.pallas import tpu as pltpu
from jax.sharding import PartitionSpec as P

GROUPS = 32
HEADS = 8
HEAD_DIM = 64
TFREQ = 64
EPSILON = 1e-05
LANES = 128
CHUNK = 64
F32 = jnp.float32
BF16 = jnp.bfloat16
MESH = pl.DeviceIdType.MESH


def sine(angle):
    turns = jnp.floor(angle * (0.5 / math.pi) + 0.5)
    x = (angle - turns * 6.28125) - turns * (2.0 * math.pi - 6.28125)
    square = x * x
    total = jnp.full_like(x, 1.0 / math.factorial(17))
    for power in (15, 13, 11, 9, 7, 5, 3, 1):
        sign = -1.0 if (power // 2) % 2 else 1.0
        total = total * square + sign / math.factorial(power)
    return total * x


def group_totals(tile, size):
    lane = lax.broadcasted_iota(jnp.int32, tile.shape, 1)
    step = 1
    while step < size:
        up = pltpu.roll(tile, LANES - step, axis=1)
        down = pltpu.roll(tile, step, axis=1)
        tile = tile + jnp.where(lane % (2 * step) < step, up, down)
        step *= 2
    return tile


def wide(tile):
    return jnp.concatenate([tile[i : i + 1] for i in range(tile.shape[0])], axis=1)


def kernel(
    n, feat, conv_first, conv_second, query_w, key_w, value_w, output_w, time_w, gains, shifts,
    text, timestep, aug_level, text_length, out,
    x, w1, w2, wq, wk, wv, wo, wt, txt, a3, y, hid, hsend, halo1, halo2, blk, kb, vb, ones, film,
    st_send, st_recv, load_sem, st_s, st_r, halo_s, halo_r,
):
    images, band, cols, channels = feat.shape
    tokens = text.shape[1]
    cells = band * cols
    tiles = channels // LANES
    per_group = channels // GROUPS
    count = float(cells * n * per_group)
    me = lax.axis_index("rows")

    loads = [
        pltpu.make_async_copy(src, dst, load_sem.at[i])
        for i, (src, dst) in enumerate(
            [(feat.at[i], x.at[i]) for i in range(images)]
            + [(text, txt), (key_w, wk), (value_w, wv), (time_w, wt), (conv_first, w1)]
            + [(conv_second, w2), (query_w, wq), (output_w, wo)]
        )
    ]
    for load in loads:
        load.start()
    text_load, key_load, value_load, time_load, first_load, second_load, query_load, out_load = (
        loads[images:]
    )

    barrier = pltpu.get_barrier_semaphore()
    for d in range(1, n):
        pl.semaphore_signal(
            barrier, inc=1, device_id={"rows": lax.rem(me + d, n)}, device_id_type=MESH
        )

    def stat_copies(phase, first, size):
        slot = 0 if phase == 0 else 1 + first - images
        return [
            pltpu.make_async_remote_copy(
                src_ref=st_send.at[pl.ds(first, size)],
                dst_ref=st_recv.at[d, pl.ds(first, size)],
                send_sem=st_s.at[slot, d],
                recv_sem=st_r.at[slot, d],
                device_id={"rows": lax.rem(me + d, n)},
                device_id_type=MESH,
            )
            for d in range(1, n)
        ]

    def halo_copy(phase, image, way, src, halo):
        return pltpu.make_async_remote_copy(
            src_ref=src,
            dst_ref=halo.at[image, way],
            send_sem=halo_s.at[phase, image, way],
            recv_sem=halo_r.at[phase, image, way],
            device_id={"rows": me + 1 if way == 0 else me - 1},
            device_id_type=MESH,
        )

    def halo_do(phase, image, rows, halo, what):
        @pl.when(me < n - 1)
        def _():
            getattr(halo_copy(phase, image, 0, rows.at[image, band - 1], halo), what)()

        @pl.when(me > 0)
        def _():
            getattr(halo_copy(phase, image, 1, rows.at[image, 0], halo), what)()

    def norm_terms(index, image, which):
        total = st_send[index]
        for d in range(1, n):
            total = total + st_recv[d, index]
        total = group_totals(total, per_group) * (1.0 / count)
        mean, square = total[:tiles], total[tiles:]
        gain = gains[which : which + 1, :]
        scale = wide(lax.rsqrt(square - mean * mean + EPSILON)) * gain
        return scale, shifts[which : which + 1, :] - wide(mean) * scale

    def activate(read, image, scale, shift, places):
        def body(c, carry):
            start = pl.multiple_of(c * CHUNK, CHUNK)
            half = read(start).astype(F32) * scale + shift
            value = (half * jnp.tanh(half) + half).astype(BF16)
            for row, p in places:
                a3[image, pl.ds(row * cols + start, CHUNK), p * channels : (p + 1) * channels] = value
            return carry

        lax.fori_loop(0, cols // CHUNK, body, 0)

    def blank(image, row, p):
        def body(c, carry):
            start = pl.multiple_of(c * CHUNK, CHUNK)
            a3[image, pl.ds(row * cols + start, CHUNK), p * channels : (p + 1) * channels] = (
                jnp.zeros((CHUNK, channels), BF16)
            )
            return carry

        lax.fori_loop(0, cols // CHUNK, body, 0)

    def spots(row):
        return [(row - p + 1, p) for p in range(3) if 0 <= row - p + 1 < band]

    def activate_all(phase, image, read, rows, halo, scale, shift):
        scale, shift = scale * 0.5, shift * 0.5
        for row in range(band):
            activate(functools.partial(read, row), image, scale, shift, spots(row))
        for way, row, here in ((0, -1, me > 0), (1, band, me < n - 1)):
            (place,) = spots(row)

            @pl.when(here)
            def _(way=way, place=place):
                halo_copy(phase, image, way, rows.at[image, 0], halo).wait_recv()
                activate(
                    lambda start: halo[image, way, pl.ds(start, CHUNK), :],
                    image, scale, shift, [place],
                )

            @pl.when(jnp.logical_not(here))
            def _(place=place):
                blank(image, *place)

    def convolve(image, w, finish):
        for q in range(3):
            y[q] = jnp.dot(
                a3[image], w[:, q].reshape(3 * channels, channels), preferred_element_type=F32
            )
        column = lax.broadcasted_iota(jnp.int32, (cols, LANES), 0)
        sums, squares = [], []
        for tile in range(tiles):
            lanes = slice(tile * LANES, (tile + 1) * LANES)
            total, square = 0.0, 0.0
            for row in range(band):
                here = slice(row * cols, (row + 1) * cols)
                left = jnp.where(column == 0, 0.0, pltpu.roll(y[0, here, lanes], 1, axis=0))
                right = jnp.where(
                    column == cols - 1, 0.0, pltpu.roll(y[2, here, lanes], cols - 1, axis=0)
                )
                value = finish(row, here, lanes, y[1, here, lanes] + left + right)
                total = total + jnp.sum(value, axis=0, keepdims=True)
                square = square + jnp.sum(value * value, axis=0, keepdims=True)
            sums.append(total)
            squares.append(square)
        return jnp.concatenate(sums + squares, axis=0)

    for image in range(images):
        loads[image].wait()
        total = jnp.zeros((8, channels), F32)
        square = jnp.zeros((8, channels), F32)
        for row in range(band):

            def add(c, carry):
                total, square = carry
                start = pl.multiple_of(c * CHUNK, CHUNK)
                value = x[image, row, pl.ds(start, CHUNK), :].astype(F32)
                for i in range(CHUNK // 8):
                    part = value[i * 8 : (i + 1) * 8]
                    total = total + part
                    square = square + part * part
                return total, square

            total, square = lax.fori_loop(0, cols // CHUNK, add, (total, square))
        total = jnp.sum(total, axis=0, keepdims=True)
        square = jnp.sum(square, axis=0, keepdims=True)
        st_send[image] = jnp.concatenate(
            [v[:, t * LANES : (t + 1) * LANES] for v in (total, square) for t in range(tiles)],
            axis=0,
        )
    pl.semaphore_wait(barrier, n - 1)
    sent = stat_copies(0, 0, images)
    for copy in sent:
        copy.start()
    for image in range(images):
        halo_do(0, image, x, halo1, "start")

    quads = kb.shape[1]
    per_quad = HEADS // quads
    width = per_quad * HEAD_DIM
    head_of_lane = lax.broadcasted_iota(jnp.int32, (tokens, width), 1) // HEAD_DIM
    text_load.wait()
    key_load.wait()
    value_load.wait()
    for image in range(images):
        keys = jnp.dot(txt[image], wk[...], preferred_element_type=F32).astype(BF16).astype(F32)
        values = jnp.dot(txt[image], wv[...], preferred_element_type=F32)
        for quad in range(quads):
            lanes = slice(quad * width, (quad + 1) * width)
            for head in range(per_quad):
                rows = slice(head * tokens, (head + 1) * tokens)
                mine = head_of_lane == head
                kb[image, quad, rows, :] = jnp.where(
                    mine, keys[:, lanes] * HEAD_DIM**-0.5, 0.0
                ).astype(BF16)
                vb[image, quad, rows, :] = jnp.where(mine, values[:, lanes], 0.0).astype(BF16)
    for head in range(per_quad):
        ones[head * tokens : (head + 1) * tokens, :] = jnp.where(
            head_of_lane == head, 1.0, 0.0
        ).astype(BF16)
    lane = lax.broadcasted_iota(jnp.int32, (16, 4 * TFREQ), 1)
    image_of_row = lax.broadcasted_iota(jnp.int32, (16, 4 * TFREQ), 0)
    step_value = jnp.zeros((16, 4 * TFREQ), F32)
    for image in range(images):
        here = jnp.where(lane < 2 * TFREQ, timestep[image], aug_level[image]).astype(F32)
        step_value = jnp.where(image_of_row == image, here, step_value)
    angle = step_value * jnp.exp((lane % TFREQ).astype(F32) * (-math.log(10000.0) / TFREQ))
    quarter = jnp.where(lane % (2 * TFREQ) < TFREQ, 0.0, 0.5 * math.pi)
    time_load.wait()
    film[...] = jnp.dot(sine(angle + quarter).astype(BF16), wt[...], preferred_element_type=F32)

    for copy in sent:
        copy.wait_recv()
    terms = [norm_terms(image, image, 0) for image in range(images)]
    pending = list(sent)
    first_load.wait()

    for image in range(images):

        def read_x(row, start, image=image):
            return x[image, row, pl.ds(start, CHUNK), :]

        activate_all(0, image, read_x, x, halo1, *terms[image])

        def keep(row, here, lanes, value, image=image):
            hid[image, here, lanes] = value
            hsend[image, row, :, lanes] = value.astype(BF16)
            return value

        st_send[images + image] = convolve(image, w1, keep)
        sent = stat_copies(1, images + image, 1)
        for copy in sent:
            copy.start()
        pending.append(sent)
        halo_do(1, image, hsend, halo2, "start")

    second_load.wait()
    for image in range(images):
        for copy in pending[len(pending) - images]:
            copy.wait_recv()
        scale, shift = norm_terms(images + image, image, 1)
        grow = 1.0 + film[image : image + 1, :channels]
        scale, shift = scale * grow, shift * grow + film[image : image + 1, channels:]

        def read_hid(row, start, image=image):
            return hid[image, pl.ds(row * cols + start, CHUNK), :]

        activate_all(1, image, read_hid, hsend, halo2, scale, shift)

        def add_residual(row, here, lanes, value, image=image):
            rounded = (x[image, row, :, lanes].astype(F32) + value).astype(BF16)
            blk[image, here, lanes] = rounded
            return rounded.astype(F32)

        st_send[2 * images + image] = convolve(image, w2, add_residual)
        sent = stat_copies(2, 2 * images + image, 1)
        for copy in sent:
            copy.start()
        pending.append(sent)

    query_load.wait()
    out_load.wait()
    for image in range(images):
        for copy in pending[len(pending) - images + image]:
            copy.wait_recv()
        scale, shift = norm_terms(2 * images + image, image, 2)
        length = text_length[image]

        for row in range(band):
            here = slice(row * cols, (row + 1) * cols)
            block = blk[image, here, :].astype(F32)
            normed = (block * scale + shift).astype(BF16)
            queries = jnp.dot(normed, wq[...], preferred_element_type=F32).astype(BF16)
            mixed = []
            for quad in range(quads):
                scores = lax.dot_general(
                    queries[:, quad * width : (quad + 1) * width],
                    kb[image, quad],
                    (((1,), (1,)), ((), ())),
                    preferred_element_type=F32,
                )
                token = lax.broadcasted_iota(jnp.int32, (cols, tokens), 1)
                raised = []
                for head in range(per_quad):
                    score = jnp.where(
                        token < length, scores[:, head * tokens : (head + 1) * tokens], -jnp.inf
                    )
                    highest = jnp.max(score, axis=1, keepdims=True)
                    raised.append(jnp.exp(score - highest).astype(BF16))
                raised = jnp.concatenate(raised, axis=1)
                top = jnp.dot(raised, vb[image, quad], preferred_element_type=F32)
                bottom = jnp.dot(raised, ones[...], preferred_element_type=F32)
                mixed.append((top / bottom).astype(BF16))
            mixed = jnp.concatenate(mixed, axis=1)
            projected = jnp.dot(mixed, wo[...], preferred_element_type=F32)
            out[image, row] = (blk[image, here, :].astype(F32) + projected).astype(BF16)

    for item in pending:
        for copy in item if isinstance(item, list) else [item]:
            copy.wait_send()
    for image in range(images):
        halo_do(0, image, x, halo1, "wait_send")
        halo_do(1, image, hsend, halo2, "wait_send")


def shards(*args):
    features, text = args[0], args[10]
    images, band, cols, channels = features.shape
    tokens = text.shape[1]
    cells = band * cols
    n = lax.axis_size("rows")
    quads = max(1, HEADS * HEAD_DIM // 256)
    width = HEADS * HEAD_DIM // quads
    stacked = width // HEAD_DIM * tokens
    any_space = pl.BlockSpec(memory_space=pl.ANY)
    vmem = pl.BlockSpec(memory_space=pltpu.VMEM)
    smem = pl.BlockSpec(memory_space=pltpu.SMEM)
    dma = pltpu.SemaphoreType.DMA
    return pl.pallas_call(
        functools.partial(kernel, n),
        out_shape=jax.ShapeDtypeStruct(features.shape, BF16),
        in_specs=[any_space] * 8 + [vmem] * 2 + [any_space] + [smem] * 3,
        out_specs=vmem,
        scratch_shapes=[
            pltpu.VMEM(features.shape, BF16),
            pltpu.VMEM(args[1].shape, BF16),
            pltpu.VMEM(args[2].shape, BF16),
            pltpu.VMEM(args[3].shape, BF16),
            pltpu.VMEM(args[4].shape, BF16),
            pltpu.VMEM(args[5].shape, BF16),
            pltpu.VMEM(args[6].shape, BF16),
            pltpu.VMEM(args[7].shape, BF16),
            pltpu.VMEM(text.shape, BF16),
            pltpu.VMEM((images, cells, 3 * channels), BF16),
            pltpu.VMEM((3, cells, channels), F32),
            pltpu.VMEM((images, cells, channels), F32),
            pltpu.VMEM(features.shape, BF16),
            pltpu.VMEM((images, 2, cols, channels), BF16),
            pltpu.VMEM((images, 2, cols, channels), BF16),
            pltpu.VMEM((images, cells, channels), BF16),
            pltpu.VMEM((images, quads, stacked, width), BF16),
            pltpu.VMEM((images, quads, stacked, width), BF16),
            pltpu.VMEM((stacked, width), BF16),
            pltpu.VMEM((16, 2 * channels), F32),
            pltpu.VMEM((3 * images, 2 * channels // LANES, LANES), F32),
            pltpu.VMEM((n, 3 * images, 2 * channels // LANES, LANES), F32),
            dma((images + 8,)),
            dma((1 + 2 * images, n)),
            dma((1 + 2 * images, n)),
            dma((2, images, 2)),
            dma((2, images, 2)),
        ],
        compiler_params=pltpu.CompilerParams(
            collective_id=0, has_side_effects=True, vmem_limit_bytes=56 * 1024 * 1024
        ),
    )(*args)


def solution(mesh):
    placed = (
        P("img", "rows", None, None),
        P(),
        P(),
        P(),
        P(),
        P(),
        P(),
        P(),
        P(),
        P(),
        P("img", None, None),
        P("img"),
        P("img"),
        P("img"),
    )
    return jax.shard_map(
        shards, mesh=mesh, in_specs=placed, out_specs=P("img", "rows", None, None), check_vma=False
    )
```

time: 113 us -> 37.5 us (0.33)
  blocking collectives: 52.2 us -> 0 us
  Pallas kernels: 0 us -> 35 us
  matrix products: 21.4 us -> 0 us
  local copies, waits for them, and re-layouts: 19.9 us -> 2.26 us
  other arithmetic: 12.9 us -> 0 us
  starting transfers between devices: 5.4 us -> 0 us
    psum x3 -> x0, blocking collectives: 52.2 us -> none  [normalize(): lax.psum((to_groups(values.sum(axis=(1, 2))), to_groups(jnp.square(values...]
    pallas_call x0 -> x1, Pallas kernels: none -> 35 us  [shards(): pl.pallas_call(functools.partial(kernel, n), out_shape=jax.ShapeDtypeStru...]
    dot_general x13 -> x0, matrix products: 21.4 us -> none  [the longest x6 12.6 us: convolve(): jnp.dot(window, stacked[offset], preferred_element_type=jnp.float32)]
    slice x10 -> x0, local copies, waits for them, and re-layouts: 11.7 us -> none  [the longest x2 5.32 us: convolve(): stacked[offset]]
    reshape x9 -> x0, local copies, waits for them, and re-layouts: 5.49 us -> none  [the longest x1 2.84 us: cross_attend(): queries = queries.reshape(images, rows_here * col_count, HEADS, HEAD_DIM)]
    ppermute x4 -> x0, starting transfers between devices: 5.4 us -> none  [the longest x2 2.76 us: padded_2(): lax.ppermute(lax.slice_in_dim(block, 0, width, axis=dim), axis, backward)]
    concatenate x4 -> x0, other arithmetic: 5.33 us -> none  [the longest x2 3.2 us: convolve(): jnp.concatenate([padded[:, :, 0:col_count], padded[:, :, 1:col_count + 1]...]
    convert_element_type x5 -> x0, other arithmetic: 3.52 us -> none  [the longest x1 2.4 us: shards(): second_core = jax.nn.silu((normalize(hidden_one, cells_count) * norm_gain...]
  transfers between devices with their start and end apart: 4 -> 0, of which waited for: 0 -> 0; matrix products, arithmetic and copies ran while one was open for 10% -> 0% of each run, Pallas kernels for 0% -> 0%
where the time goes in v1:
time: 37.5 us; the launch traced here: 37.3 us
  Pallas kernels  35 us (93%)
  local copies, waits for them, and re-layouts  2.26 us (6%)
    pallas_call x1, Pallas kernels, shards(): pl.pallas_call(functools.partial(kernel, n), out_shape=jax.ShapeDtypeStru...  35 us
    unnamed x1, local copies, waits for them, and re-layouts  2.26 us

profile of v1, /device:TPU:0, one launch (start us, length us, event | category | flops | bytes accessed | tf_op | source)
XLA Modules:
  0.0 37.3 jit_solution(7632702895726164155)
XLA Ops:
  0.0 35.0 %shard_map.136 = bf16[2,2,256,512]{3,2,1,0:T(8,128)(2,1)} custom-call(bf16[2,2,256,512]{3,2,1,0:T(8,128)(2,1)} %feat.1, bf16[3,3,512,512]{3,2,1,0:T(8,128)(2,1)} %conv_first.1, bf16[3,3,512,512]{3,2,1,0:T(8,128)(2,1)} %conv_second.1, bf16[512,512]{1,0:T(8,128)(2,1)} %query_w.1, bf16[512,512]{1,0:T(8,128)(2,1)} %key_w.1, bf16[512,512]{1,0:T(8,128)(2,1)} %value_w.1, ...), custom_call_target="tpu_custom_call" | custom-call | tf_op jit(solution)/shard_map/pallas_call | solution.py:363
  35.0 2.3 %copy.16 = bf16[2,2,256,512]{3,2,1,0:T(8,128)(2,1)} copy(bf16[2,2,256,512]{3,2,1,0:T(8,128)(2,1)} %shard_map.136) | data formatting | bytes 2097152

commit v2 on v1

--- a/solution.py
+++ b/solution.py
@@ -15,6 +15,7 @@
 EPSILON = 1e-05
 LANES = 128
 CHUNK = 64
+STRETCH = 32
 F32 = jnp.float32
 BF16 = jnp.bfloat16
 MESH = pl.DeviceIdType.MESH
@@ -47,32 +48,23 @@
 
 
 def kernel(
-    n, feat, conv_first, conv_second, query_w, key_w, value_w, output_w, time_w, gains, shifts,
-    text, timestep, aug_level, text_length, out,
-    x, w1, w2, wq, wk, wv, wo, wt, txt, a3, y, hid, hsend, halo1, halo2, blk, kb, vb, ones, film,
+    n, x, conv_first, conv_second, wq, wk, wv, wo, wt, gains, shifts,
+    txt, timestep, aug_level, text_length, out,
+    w1, w2, a3, hid, hsend, halo1, halo2, blk, kb, vb, ones, film, affine,
     st_send, st_recv, load_sem, st_s, st_r, halo_s, halo_r,
 ):
-    images, band, cols, channels = feat.shape
-    tokens = text.shape[1]
+    images, band, cols, channels = x.shape
+    tokens = txt.shape[1]
     cells = band * cols
     tiles = channels // LANES
     per_group = channels // GROUPS
     count = float(cells * n * per_group)
     me = lax.axis_index("rows")
 
-    loads = [
-        pltpu.make_async_copy(src, dst, load_sem.at[i])
-        for i, (src, dst) in enumerate(
-            [(feat.at[i], x.at[i]) for i in range(images)]
-            + [(text, txt), (key_w, wk), (value_w, wv), (time_w, wt), (conv_first, w1)]
-            + [(conv_second, w2), (query_w, wq), (output_w, wo)]
-        )
-    ]
-    for load in loads:
-        load.start()
-    text_load, key_load, value_load, time_load, first_load, second_load, query_load, out_load = (
-        loads[images:]
-    )
+    first_load = pltpu.make_async_copy(conv_first, w1, load_sem.at[0])
+    second_load = pltpu.make_async_copy(conv_second, w2, load_sem.at[1])
+    first_load.start()
+    second_load.start()
 
     barrier = pltpu.get_barrier_semaphore()
     for d in range(1, n):
@@ -123,74 +115,84 @@
         scale = wide(lax.rsqrt(square - mean * mean + EPSILON)) * gain
         return scale, shifts[which : which + 1, :] - wide(mean) * scale
 
-    def activate(read, image, scale, shift, places):
-        def body(c, carry):
-            start = pl.multiple_of(c * CHUNK, CHUNK)
-            half = read(start).astype(F32) * scale + shift
-            value = (half * jnp.tanh(half) + half).astype(BF16)
-            for row, p in places:
-                a3[image, pl.ds(row * cols + start, CHUNK), p * channels : (p + 1) * channels] = value
+    def place_at(row, p, q, lane):
+        start = pl.multiple_of((p * 3 + q) * channels + lane, LANES)
+        return slice(row * cols, (row + 1) * cols), pl.ds(start, LANES)
+
+    def activate(read, image, places):
+        def body(tile, carry):
+            lane = pl.multiple_of(tile * LANES, LANES)
+            column = lax.broadcasted_iota(jnp.int32, (cols, LANES), 0)
+            half = read(lane).astype(F32) * affine[0:1, pl.ds(lane, LANES)]
+            half = half + affine[1:2, pl.ds(lane, LANES)]
+            value = half * jnp.tanh(half) + half
+            left = jnp.where(column == 0, 0.0, pltpu.roll(value, 1, axis=0))
+            right = jnp.where(column == cols - 1, 0.0, pltpu.roll(value, cols - 1, axis=0))
+            for q, tap in enumerate((left, value, right)):
+                tap = tap.astype(BF16)
+                for row, p in places:
+                    rows, lanes = place_at(row, p, q, lane)
+                    a3[image, rows, lanes] = tap
             return carry
 
-        lax.fori_loop(0, cols // CHUNK, body, 0)
+        lax.fori_loop(0, tiles, body, 0)
 
     def blank(image, row, p):
-        def body(c, carry):
-            start = pl.multiple_of(c * CHUNK, CHUNK)
-            a3[image, pl.ds(row * cols + start, CHUNK), p * channels : (p + 1) * channels] = (
-                jnp.zeros((CHUNK, channels), BF16)
-            )
-            return carry
-
-        lax.fori_loop(0, cols // CHUNK, body, 0)
+        a3[image, row * cols : (row + 1) * cols, 3 * p * channels : 3 * (p + 1) * channels] = (
+            jnp.zeros((cols, 3 * channels), BF16)
+        )
 
     def spots(row):
         return [(row - p + 1, p) for p in range(3) if 0 <= row - p + 1 < band]
 
     def activate_all(phase, image, read, rows, halo, scale, shift):
-        scale, shift = scale * 0.5, shift * 0.5
+        affine[0:1, :] = scale * 0.5
+        affine[1:2, :] = shift * 0.5
         for row in range(band):
-            activate(functools.partial(read, row), image, scale, shift, spots(row))
+            activate(functools.partial(read, row), image, spots(row))
         for way, row, here in ((0, -1, me > 0), (1, band, me < n - 1)):
             (place,) = spots(row)
 
             @pl.when(here)
             def _(way=way, place=place):
                 halo_copy(phase, image, way, rows.at[image, 0], halo).wait_recv()
-                activate(
-                    lambda start: halo[image, way, pl.ds(start, CHUNK), :],
-                    image, scale, shift, [place],
-                )
+                activate(lambda lane: halo[image, way, :, pl.ds(lane, LANES)], image, [place])
 
             @pl.when(jnp.logical_not(here))
             def _(place=place):
                 blank(image, *place)
 
     def convolve(image, w, finish):
-        for q in range(3):
-            y[q] = jnp.dot(
-                a3[image], w[:, q].reshape(3 * channels, channels), preferred_element_type=F32
-            )
-        column = lax.broadcasted_iota(jnp.int32, (cols, LANES), 0)
-        sums, squares = [], []
-        for tile in range(tiles):
-            lanes = slice(tile * LANES, (tile + 1) * LANES)
-            total, square = 0.0, 0.0
-            for row in range(band):
-                here = slice(row * cols, (row + 1) * cols)
-                left = jnp.where(column == 0, 0.0, pltpu.roll(y[0, here, lanes], 1, axis=0))
-                right = jnp.where(
-                    column == cols - 1, 0.0, pltpu.roll(y[2, here, lanes], cols - 1, axis=0)
-                )
-                value = finish(row, here, lanes, y[1, here, lanes] + left + right)
-                total = total + jnp.sum(value, axis=0, keepdims=True)
-                square = square + jnp.sum(value * value, axis=0, keepdims=True)
-            sums.append(total)
-            squares.append(square)
-        return jnp.concatenate(sums + squares, axis=0)
-
-    for image in range(images):
-        loads[image].wait()
+        hid[image] = jnp.dot(
+            a3[image], w[...].reshape(9 * channels, channels), preferred_element_type=F32
+        )
+        total = jnp.zeros((8, channels), F32)
+        square = jnp.zeros((8, channels), F32)
+        for row in range(band):
+
+            def add(c, carry, row=row):
+                total, square = carry
+                start = pl.multiple_of(c * STRETCH, STRETCH)
+                here = pl.ds(row * cols + start, STRETCH)
+                value = finish(row, pl.ds(start, STRETCH), here, hid[image, here, :])
+                for i in range(STRETCH // 8):
+                    part = value[i * 8 : (i + 1) * 8]
+                    total = total + part
+                    square = square + part * part
+                return total, square
+
+            total, square = lax.fori_loop(0, cols // STRETCH, add, (total, square))
+        return stat_tile(total, square)
+
+    def stat_tile(total, square):
+        total = jnp.sum(total, axis=0, keepdims=True)
+        square = jnp.sum(square, axis=0, keepdims=True)
+        return jnp.concatenate(
+            [v[:, t * LANES : (t + 1) * LANES] for v in (total, square) for t in range(tiles)],
+            axis=0,
+        )
+
+    for image in range(images):
         total = jnp.zeros((8, channels), F32)
         square = jnp.zeros((8, channels), F32)
         for row in range(band):
@@ -206,12 +208,7 @@
                 return total, square
 
             total, square = lax.fori_loop(0, cols // CHUNK, add, (total, square))
-        total = jnp.sum(total, axis=0, keepdims=True)
-        square = jnp.sum(square, axis=0, keepdims=True)
-        st_send[image] = jnp.concatenate(
-            [v[:, t * LANES : (t + 1) * LANES] for v in (total, square) for t in range(tiles)],
-            axis=0,
-        )
+        st_send[image] = stat_tile(total, square)
     pl.semaphore_wait(barrier, n - 1)
     sent = stat_copies(0, 0, images)
     for copy in sent:
@@ -223,9 +220,6 @@
     per_quad = HEADS // quads
     width = per_quad * HEAD_DIM
     head_of_lane = lax.broadcasted_iota(jnp.int32, (tokens, width), 1) // HEAD_DIM
-    text_load.wait()
-    key_load.wait()
-    value_load.wait()
     for image in range(images):
         keys = jnp.dot(txt[image], wk[...], preferred_element_type=F32).astype(BF16).astype(F32)
         values = jnp.dot(txt[image], wv[...], preferred_element_type=F32)
@@ -250,7 +244,6 @@
         step_value = jnp.where(image_of_row == image, here, step_value)
     angle = step_value * jnp.exp((lane % TFREQ).astype(F32) * (-math.log(10000.0) / TFREQ))
     quarter = jnp.where(lane % (2 * TFREQ) < TFREQ, 0.0, 0.5 * math.pi)
-    time_load.wait()
     film[...] = jnp.dot(sine(angle + quarter).astype(BF16), wt[...], preferred_element_type=F32)
 
     for copy in sent:
@@ -261,14 +254,13 @@
 
     for image in range(images):
 
-        def read_x(row, start, image=image):
-            return x[image, row, pl.ds(start, CHUNK), :]
+        def read_x(row, lane, image=image):
+            return x[image, row, :, pl.ds(lane, LANES)]
 
         activate_all(0, image, read_x, x, halo1, *terms[image])
 
-        def keep(row, here, lanes, value, image=image):
-            hid[image, here, lanes] = value
-            hsend[image, row, :, lanes] = value.astype(BF16)
+        def keep(row, columns, here, value, image=image):
+            hsend[image, row, columns, :] = value.astype(BF16)
             return value
 
         st_send[images + image] = convolve(image, w1, keep)
@@ -286,14 +278,14 @@
         grow = 1.0 + film[image : image + 1, :channels]
         scale, shift = scale * grow, shift * grow + film[image : image + 1, channels:]
 
-        def read_hid(row, start, image=image):
-            return hid[image, pl.ds(row * cols + start, CHUNK), :]
+        def read_hid(row, lane, image=image):
+            return hid[image, row * cols : (row + 1) * cols, pl.ds(lane, LANES)]
 
         activate_all(1, image, read_hid, hsend, halo2, scale, shift)
 
-        def add_residual(row, here, lanes, value, image=image):
-            rounded = (x[image, row, :, lanes].astype(F32) + value).astype(BF16)
-            blk[image, here, lanes] = rounded
+        def add_residual(row, columns, here, value, image=image):
+            rounded = (x[image, row, columns, :].astype(F32) + value).astype(BF16)
+            blk[image, here, :] = rounded
             return rounded.astype(F32)
 
         st_send[2 * images + image] = convolve(image, w2, add_residual)
@@ -302,8 +294,6 @@
             copy.start()
         pending.append(sent)
 
-    query_load.wait()
-    out_load.wait()
     for image in range(images):
         for copy in pending[len(pending) - images + image]:
             copy.wait_recv()
@@ -363,20 +353,12 @@
     return pl.pallas_call(
         functools.partial(kernel, n),
         out_shape=jax.ShapeDtypeStruct(features.shape, BF16),
-        in_specs=[any_space] * 8 + [vmem] * 2 + [any_space] + [smem] * 3,
+        in_specs=[vmem] + [any_space] * 2 + [vmem] * 8 + [smem] * 3,
         out_specs=vmem,
         scratch_shapes=[
-            pltpu.VMEM(features.shape, BF16),
             pltpu.VMEM(args[1].shape, BF16),
             pltpu.VMEM(args[2].shape, BF16),
-            pltpu.VMEM(args[3].shape, BF16),
-            pltpu.VMEM(args[4].shape, BF16),
-            pltpu.VMEM(args[5].shape, BF16),
-            pltpu.VMEM(args[6].shape, BF16),
-            pltpu.VMEM(args[7].shape, BF16),
-            pltpu.VMEM(text.shape, BF16),
-            pltpu.VMEM((images, cells, 3 * channels), BF16),
-            pltpu.VMEM((3, cells, channels), F32),
+            pltpu.VMEM((images, cells, 9 * channels), BF16),
             pltpu.VMEM((images, cells, channels), F32),
             pltpu.VMEM(features.shape, BF16),
             pltpu.VMEM((images, 2, cols, channels), BF16),
@@ -386,16 +368,17 @@
             pltpu.VMEM((images, quads, stacked, width), BF16),
             pltpu.VMEM((stacked, width), BF16),
             pltpu.VMEM((16, 2 * channels), F32),
+            pltpu.VMEM((8, channels), F32),
             pltpu.VMEM((3 * images, 2 * channels // LANES, LANES), F32),
             pltpu.VMEM((n, 3 * images, 2 * channels // LANES, LANES), F32),
-            dma((images + 8,)),
+            dma((2,)),
             dma((1 + 2 * images, n)),
             dma((1 + 2 * images, n)),
             dma((2, images, 2)),
             dma((2, images, 2)),
         ],
         compiler_params=pltpu.CompilerParams(
-            collective_id=0, has_side_effects=True, vmem_limit_bytes=56 * 1024 * 1024
+            collective_id=0, has_side_effects=True, vmem_limit_bytes=48 * 1024 * 1024
         ),
     )(*args)
 

time: 37.5 us -> 47.8 us (1.27)
  local copies, waits for them, and re-layouts: 2.26 us -> 11.7 us
  Pallas kernels: 35 us -> 35.5 us
    unnamed x1 -> x25, local copies, waits for them, and re-layouts: 2.26 us -> 11.7 us
    pallas_call x1, Pallas kernels: 35 us -> 35.5 us  [shards(): pl.pallas_call(functools.partial(kernel, n), out_shape=jax.ShapeDtypeStru...]
where the time goes in v2:
time: 47.8 us; the launch traced here: 47.2 us
  Pallas kernels  35.5 us (74%)
  local copies, waits for them, and re-layouts  11.7 us (24%)
    pallas_call x1, Pallas kernels, shards(): pl.pallas_call(functools.partial(kernel, n), out_shape=jax.ShapeDtypeStru...  35.5 us
    unnamed x25, local copies, waits for them, and re-layouts  11.7 us

profile of v2, /device:TPU:0, one launch (start us, length us, event | category | flops | bytes accessed | tf_op | source)
XLA Modules:
  0.0 47.2 jit_solution(680499574241924259)
XLA Ops:
  0.0 0.0 copy-start
  0.0 1.2 %copy-done = bf16[2,2,256,512]{3,2,1,0:T(8,128)(2,1)S(1)} copy-done((bf16[2,2,256,512]{3,2,1,0:T(8,128)(2,1)S(1)}, bf16[2,2,256,512]{3,2,1,0:T(8,128)(2,1)}, u32[]{:S(2)}) %copy-start) | copy-done | bytes 1048600
  1.2 0.0 copy-start.1
  1.2 1.0 %copy-done.1 = bf16[512,512]{1,0:T(8,128)(2,1)S(1)} copy-done((bf16[512,512]{1,0:T(8,128)(2,1)S(1)}, bf16[512,512]{1,0:T(8,128)(2,1)}, u32[]{:S(2)}) %copy-start.1) | copy-done | bytes 524312
  2.3 0.0 copy-start.2
  2.3 1.0 %copy-done.2 = bf16[512,512]{1,0:T(8,128)(2,1)S(1)} copy-done((bf16[512,512]{1,0:T(8,128)(2,1)S(1)}, bf16[512,512]{1,0:T(8,128)(2,1)}, u32[]{:S(2)}) %copy-start.2) | copy-done | bytes 524312
  3.3 0.0 copy-start.3
  3.3 1.0 %copy-done.3 = bf16[512,512]{1,0:T(8,128)(2,1)S(1)} copy-done((bf16[512,512]{1,0:T(8,128)(2,1)S(1)}, bf16[512,512]{1,0:T(8,128)(2,1)}, u32[]{:S(2)}) %copy-start.3) | copy-done | bytes 524312
  4.4 0.0 copy-start.4
  4.4 1.0 %copy-done.4 = bf16[512,512]{1,0:T(8,128)(2,1)S(1)} copy-done((bf16[512,512]{1,0:T(8,128)(2,1)S(1)}, bf16[512,512]{1,0:T(8,128)(2,1)}, u32[]{:S(2)}) %copy-start.4) | copy-done | bytes 524312
  5.4 0.0 copy-start.5
  5.4 1.0 %copy-done.5 = bf16[256,1024]{1,0:T(8,128)(2,1)S(1)} copy-done((bf16[256,1024]{1,0:T(8,128)(2,1)S(1)}, bf16[256,1024]{1,0:T(8,128)(2,1)}, u32[]{:S(2)}) %copy-start.5) | copy-done | bytes 524312
  6.4 0.0 copy-start.6
  6.4 0.9 %copy-done.6 = bf16[2,128,512]{2,1,0:T(8,128)(2,1)S(1)} copy-done((bf16[2,128,512]{2,1,0:T(8,128)(2,1)S(1)}, bf16[2,128,512]{2,1,0:T(8,128)(2,1)}, u32[]{:S(2)}) %copy-start.6) | copy-done | bytes 262168
  7.4 0.0 copy-start.7
  7.4 0.7 %copy-done.7 = f32[3,512]{1,0:T(4,128)S(1)} copy-done((f32[3,512]{1,0:T(4,128)S(1)}, f32[3,512]{1,0:T(4,128)}, u32[]{:S(2)}) %copy-start.7) | copy-done | bytes 6168
  8.1 0.0 copy-start.8
  8.1 0.7 %copy-done.8 = f32[3,512]{1,0:T(4,128)S(1)} copy-done((f32[3,512]{1,0:T(4,128)S(1)}, f32[3,512]{1,0:T(4,128)}, u32[]{:S(2)}) %copy-start.8) | copy-done | bytes 6168
  8.8 0.0 copy-start.9
  8.8 0.7 %copy-done.9 = s32[2]{0:T(128)S(1)} copy-done((s32[2]{0:T(128)S(1)}, s32[2]{0:T(128)}, u32[]{:S(2)}) %copy-start.9) | copy-done | bytes 32
  9.4 0.0 copy-start.10
  9.4 0.7 %copy-done.10 = s32[2]{0:T(128)S(1)} copy-done((s32[2]{0:T(128)S(1)}, s32[2]{0:T(128)}, u32[]{:S(2)}) %copy-start.10) | copy-done | bytes 32
  10.1 0.0 copy-start.11
  10.1 0.7 %copy-done.11 = s32[2]{0:T(128)S(1)} copy-done((s32[2]{0:T(128)S(1)}, s32[2]{0:T(128)}, u32[]{:S(2)}) %copy-start.11) | copy-done | bytes 32
  10.7 35.5 %shard_map.136 = bf16[2,2,256,512]{3,2,1,0:T(8,128)(2,1)S(1)} custom-call(bf16[2,2,256,512]{3,2,1,0:T(8,128)(2,1)S(1)} %copy-done, bf16[3,3,512,512]{3,2,1,0:T(8,128)(2,1)} %conv_first.1, bf16[3,3,512,512]{3,2,1,0:T(8,128)(2,1)} %conv_second.1, bf16[512,512]{1,0:T(8,128)(2,1)S(1)} %copy-done.1, bf16[512,512]{1,0:T(8,128)(2,1)S(1)} %copy-done.2, ...), custom_call_target="tpu_custom_call" | custom-call | tf_op jit(solution)/shard_map/pallas_call | solution.py:353
  46.3 1.0 %copy.16 = bf16[2,2,256,512]{3,2,1,0:T(8,128)(2,1)} copy(bf16[2,2,256,512]{3,2,1,0:T(8,128)(2,1)S(1)} %shard_map.136) | data formatting | bytes 2097152
Async XLA Ops:
  0.0 1.2 %copy-start = (bf16[2,2,256,512]{3,2,1,0:T(8,128)(2,1)S(1)}, bf16[2,2,256,512]{3,2,1,0:T(8,128)(2,1)}, u32[]{:S(2)}) copy-start(bf16[2,2,256,512]{3,2,1,0:T(8,128)(2,1)} %x.1) | copy-start | bytes 3145732
  1.2 1.0 %copy-start.1 = (bf16[512,512]{1,0:T(8,128)(2,1)S(1)}, bf16[512,512]{1,0:T(8,128)(2,1)}, u32[]{:S(2)}) copy-start(bf16[512,512]{1,0:T(8,128)(2,1)} %wq.1) | copy-start | bytes 1572868
  2.3 1.0 %copy-start.2 = (bf16[512,512]{1,0:T(8,128)(2,1)S(1)}, bf16[512,512]{1,0:T(8,128)(2,1)}, u32[]{:S(2)}) copy-start(bf16[512,512]{1,0:T(8,128)(2,1)} %wk.1) | copy-start | bytes 1572868
  3.3 1.0 %copy-start.3 = (bf16[512,512]{1,0:T(8,128)(2,1)S(1)}, bf16[512,512]{1,0:T(8,128)(2,1)}, u32[]{:S(2)}) copy-start(bf16[512,512]{1,0:T(8,128)(2,1)} %wv.1) | copy-start | bytes 1572868
  4.4 1.0 %copy-start.4 = (bf16[512,512]{1,0:T(8,128)(2,1)S(1)}, bf16[512,512]{1,0:T(8,128)(2,1)}, u32[]{:S(2)}) copy-start(bf16[512,512]{1,0:T(8,128)(2,1)} %wo.1) | copy-start | bytes 1572868
  5.4 1.0 %copy-start.5 = (bf16[256,1024]{1,0:T(8,128)(2,1)S(1)}, bf16[256,1024]{1,0:T(8,128)(2,1)}, u32[]{:S(2)}) copy-start(bf16[256,1024]{1,0:T(8,128)(2,1)} %wt.1) | copy-start | bytes 1572868
  6.4 0.9 %copy-start.6 = (bf16[2,128,512]{2,1,0:T(8,128)(2,1)S(1)}, bf16[2,128,512]{2,1,0:T(8,128)(2,1)}, u32[]{:S(2)}) copy-start(bf16[2,128,512]{2,1,0:T(8,128)(2,1)} %txt.1) | copy-start | bytes 786436
  7.4 0.7 %copy-start.7 = (f32[3,512]{1,0:T(4,128)S(1)}, f32[3,512]{1,0:T(4,128)}, u32[]{:S(2)}) copy-start(f32[3,512]{1,0:T(4,128)} %gains.1) | copy-start | bytes 18436
  8.1 0.7 %copy-start.8 = (f32[3,512]{1,0:T(4,128)S(1)}, f32[3,512]{1,0:T(4,128)}, u32[]{:S(2)}) copy-start(f32[3,512]{1,0:T(4,128)} %shifts.1) | copy-start | bytes 18436
  8.8 0.7 %copy-start.9 = (s32[2]{0:T(128)S(1)}, s32[2]{0:T(128)}, u32[]{:S(2)}) copy-start(s32[2]{0:T(128)} %timestep.1) | copy-start | bytes 28
  9.4 0.7 %copy-start.10 = (s32[2]{0:T(128)S(1)}, s32[2]{0:T(128)}, u32[]{:S(2)}) copy-start(s32[2]{0:T(128)} %aug_level.1) | copy-start | bytes 28
  10.1 0.7 %copy-start.11 = (s32[2]{0:T(128)S(1)}, s32[2]{0:T(128)}, u32[]{:S(2)}) copy-start(s32[2]{0:T(128)} %text_length.1) | copy-start | bytes 28

commit v3 on v1

--- a/solution.py
+++ b/solution.py
@@ -40,6 +40,25 @@
         tile = tile + jnp.where(lane % (2 * step) < step, up, down)
         step *= 2
     return tile
+
+
+def pack(tile, tiles, size):
+    tile = group_totals(tile, size)
+    lane = lax.broadcasted_iota(jnp.int32, tile.shape, 1)
+    row = lax.broadcasted_iota(jnp.int32, tile.shape, 0)
+    mine = jnp.where(lane % tiles == row % tiles, tile, 0.0)
+    return jnp.concatenate(
+        [jnp.sum(mine[i * tiles : (i + 1) * tiles], axis=0, keepdims=True) for i in range(2)], axis=0
+    )
+
+
+def unpack(packed, tiles):
+    tile = jnp.concatenate(
+        [jnp.broadcast_to(packed[i : i + 1], (tiles, LANES)) for i in range(2)], axis=0
+    )
+    lane = lax.broadcasted_iota(jnp.int32, tile.shape, 1)
+    row = lax.broadcasted_iota(jnp.int32, tile.shape, 0)
+    return group_totals(jnp.where(lane % tiles == row % tiles, tile, 0.0), tiles)
 
 
 def wide(tile):
@@ -117,7 +136,7 @@
         total = st_send[index]
         for d in range(1, n):
             total = total + st_recv[d, index]
-        total = group_totals(total, per_group) * (1.0 / count)
+        total = unpack(total, tiles) * (1.0 / count)
         mean, square = total[:tiles], total[tiles:]
         gain = gains[which : which + 1, :]
         scale = wide(lax.rsqrt(square - mean * mean + EPSILON)) * gain
@@ -147,10 +166,11 @@
     def spots(row):
         return [(row - p + 1, p) for p in range(3) if 0 <= row - p + 1 < band]
 
-    def activate_all(phase, image, read, rows, halo, scale, shift):
-        scale, shift = scale * 0.5, shift * 0.5
+    def activate_own(image, read, scale, shift):
         for row in range(band):
-            activate(functools.partial(read, row), image, scale, shift, spots(row))
+            activate(functools.partial(read, row), image, scale * 0.5, shift * 0.5, spots(row))
+
+    def activate_halo(phase, image, rows, halo, scale, shift):
         for way, row, here in ((0, -1, me > 0), (1, band, me < n - 1)):
             (place,) = spots(row)
 
@@ -159,7 +179,7 @@
                 halo_copy(phase, image, way, rows.at[image, 0], halo).wait_recv()
                 activate(
                     lambda start: halo[image, way, pl.ds(start, CHUNK), :],
-                    image, scale, shift, [place],
+                    image, scale * 0.5, shift * 0.5, [place],
                 )
 
             @pl.when(jnp.logical_not(here))
@@ -187,7 +207,7 @@
                 square = square + jnp.sum(value * value, axis=0, keepdims=True)
             sums.append(total)
             squares.append(square)
-        return jnp.concatenate(sums + squares, axis=0)
+        return pack(jnp.concatenate(sums + squares, axis=0), tiles, per_group)
 
     for image in range(images):
         loads[image].wait()
@@ -208,10 +228,11 @@
             total, square = lax.fori_loop(0, cols // CHUNK, add, (total, square))
         total = jnp.sum(total, axis=0, keepdims=True)
         square = jnp.sum(square, axis=0, keepdims=True)
-        st_send[image] = jnp.concatenate(
+        packed = jnp.concatenate(
             [v[:, t * LANES : (t + 1) * LANES] for v in (total, square) for t in range(tiles)],
             axis=0,
         )
+        st_send[image] = pack(packed, tiles, per_group)
     pl.semaphore_wait(barrier, n - 1)
     sent = stat_copies(0, 0, images)
     for copy in sent:
@@ -257,14 +278,17 @@
         copy.wait_recv()
     terms = [norm_terms(image, image, 0) for image in range(images)]
     pending = list(sent)
-    first_load.wait()
 
     for image in range(images):
 
         def read_x(row, start, image=image):
             return x[image, row, pl.ds(start, CHUNK), :]
 
-        activate_all(0, image, read_x, x, halo1, *terms[image])
+        activate_own(image, read_x, *terms[image])
+
+    first_load.wait()
+    for image in range(images):
+        activate_halo(0, image, x, halo1, *terms[image])
 
         def keep(row, here, lanes, value, image=image):
             hid[image, here, lanes] = value
@@ -289,7 +313,8 @@
         def read_hid(row, start, image=image):
             return hid[image, pl.ds(row * cols + start, CHUNK), :]
 
-        activate_all(1, image, read_hid, hsend, halo2, scale, shift)
+        activate_own(image, read_hid, scale, shift)
+        activate_halo(1, image, hsend, halo2, scale, shift)
 
         def add_residual(row, here, lanes, value, image=image):
             rounded = (x[image, row, :, lanes].astype(F32) + value).astype(BF16)
@@ -386,8 +411,8 @@
             pltpu.VMEM((images, quads, stacked, width), BF16),
             pltpu.VMEM((stacked, width), BF16),
             pltpu.VMEM((16, 2 * channels), F32),
-            pltpu.VMEM((3 * images, 2 * channels // LANES, LANES), F32),
-            pltpu.VMEM((n, 3 * images, 2 * channels // LANES, LANES), F32),
+            pltpu.VMEM((3 * images, 2, LANES), F32),
+            pltpu.VMEM((n, 3 * images, 2, LANES), F32),
             dma((images + 8,)),
             dma((1 + 2 * images, n)),
             dma((1 + 2 * images, n)),

time: 37.5 us -> 37.9 us (1.011)
  Pallas kernels: 35 us -> 35.4 us
    pallas_call x1, Pallas kernels: 35 us -> 35.4 us  [shards(): pl.pallas_call(functools.partial(kernel, n), out_shape=jax.ShapeDtypeStru...]
where the time goes in v3:
time: 37.9 us; the launch traced here: 37.7 us
  Pallas kernels  35.4 us (93%)
  local copies, waits for them, and re-layouts  2.26 us (6%)
    pallas_call x1, Pallas kernels, shards(): pl.pallas_call(functools.partial(kernel, n), out_shape=jax.ShapeDtypeStru...  35.4 us
    unnamed x1, local copies, waits for them, and re-layouts  2.26 us

profile of v3, /device:TPU:0, one launch (start us, length us, event | category | flops | bytes accessed | tf_op | source)
XLA Modules:
  0.0 37.7 jit_solution(4596138701558513266)
XLA Ops:
  0.0 35.4 %shard_map.136 = bf16[2,2,256,512]{3,2,1,0:T(8,128)(2,1)} custom-call(bf16[2,2,256,512]{3,2,1,0:T(8,128)(2,1)} %feat.1, bf16[3,3,512,512]{3,2,1,0:T(8,128)(2,1)} %conv_first.1, bf16[3,3,512,512]{3,2,1,0:T(8,128)(2,1)} %conv_second.1, bf16[512,512]{1,0:T(8,128)(2,1)} %query_w.1, bf16[512,512]{1,0:T(8,128)(2,1)} %key_w.1, bf16[512,512]{1,0:T(8,128)(2,1)} %value_w.1, ...), custom_call_target="tpu_custom_call" | custom-call | tf_op jit(solution)/shard_map/pallas_call | solution.py:388
  35.4 2.3 %copy.16 = bf16[2,2,256,512]{3,2,1,0:T(8,128)(2,1)} copy(bf16[2,2,256,512]{3,2,1,0:T(8,128)(2,1)} %shard_map.136) | data formatting | bytes 2097152
